TPU v7x, 32 devices: a whole 2x2x4 slice. The times are simulated.
32 devices in a mesh: perm: 2 (over y), subj: 8 (over z, core), vert: 2 (over x).
Axes of the slice: x: 2, y: 2, z: 4, core: 2. Of those that a mesh axis runs over, the one named last changes fastest.
Arguments:
- kinship: bfloat16 [2048, 2048], P('subj')
- phenotype: bfloat16 [2048, 2048], P('subj', 'vert')
- shuffle: int32 [4096], P(('perm', 'subj')), parts along dimension 0, may hold values from 0 to 2047, as said below
Outputs:
- statistic: float32 [4096], P(('perm', 'vert')), parts along dimension 0
There are 2 independent parts, one for each index of `perm`. A program takes and returns all parts, laid end to end along the dimension named above; an argument that names none is the same for every part. Nothing has to cross between parts.
Inputs may be any that keep to these rules, and one draw needn't show every extreme that they name: shuffle is a permutation of 0 to 2047 that maps every subject into its own exchangeability block.
All inputs are finite; a program needn't handle non-finite values.
Results may differ from a plain program's by a relative error of at most 0.0003.
Values may be sent and summed in bfloat16 or wider, within the bound.
A program may use at most 128 MiB of HBM per device.

v0:
```python
import jax
import jax.numpy as jnp
from jax import lax
from jax.sharding import PartitionSpec as P


def per_device(kinship, phenotype, shuffle):
    row_count = phenotype.shape[0]
    subject_count = kinship.shape[1]
    row_offset = lax.axis_index("subj") * row_count
    shuffle_all = lax.all_gather(shuffle, "subj", axis=0, tiled=True)
    own_block = lax.dynamic_slice_in_dim(kinship, row_offset, row_count, 1)
    kin_diag = jnp.diagonal(own_block).astype(jnp.float32)
    inverse = (
        jnp.zeros((subject_count,), jnp.int32)
        .at[shuffle_all]
        .set(jnp.arange(subject_count, dtype=jnp.int32))
    )
    kin_moved = jnp.take(kinship, inverse, axis=1)
    piece = lax.all_gather(phenotype, "subj", axis=0, tiled=True)
    piece_rows = piece.shape[0]
    targets = jnp.arange(piece_rows, dtype=jnp.int32)
    picker = (shuffle[:, None] == targets[None, :]).astype(jnp.bfloat16)
    product = jnp.dot(kin_moved, piece, preferred_element_type=jnp.float32)
    picked = jnp.dot(picker, piece, preferred_element_type=jnp.float32)
    local_perm = picked.astype(jnp.bfloat16)
    moved = local_perm.astype(jnp.float32)
    cross_term = jnp.sum(moved * (product - kin_diag[:, None] * moved), axis=0)
    values = phenotype.astype(jnp.float32)
    squares = jnp.sum(values * values, axis=0)
    cross_all, squares_all = lax.psum((cross_term, squares), "subj")
    return cross_all / (
        jnp.sqrt(jnp.float32(subject_count)) * (squares_all / subject_count + 1e-05)
    )


def solution(mesh):
    in_specs = (P("subj", None), P("subj", "vert"), P(("perm", "subj")))
    out_specs = P(("perm", "vert"))
    return jax.shard_map(
        per_device, mesh=mesh, in_specs=in_specs, out_specs=out_specs, check_vma=False
    )
```

profile of v0, /device:TPU:0, one launch (start us, length us, event | category | flops | bytes accessed | tf_op | source)
XLA Modules:
  0.0 86.2 jit_solution(4435707539312031258)
XLA Ops:
  6.5 0.0 all-gather.3.cloned.1.call-start
  6.5 0.7 all-gather.3.cloned.1.call-update
  7.3 1.5 %copy.6 = bf16[256,2048]{0,1:T(8,128)(2,1)S(1)} copy(bf16[256,2048]{1,0:T(8,128)(2,1)} %param.3) | data formatting | bytes 2097152 | tf_op args[0]
  8.8 0.9 %constant_dynamic-slice_fusion = bf16[256,256]{1,0:T(8,128)(2,1)S(1)} fusion(bf16[256,2048]{1,0:T(8,128)(2,1)} %param.3, s32[]{:T(128)S(6)} %select_n.22), kind=kLoop, calls=%fused_computation.23 | loop fusion | bytes 262148 | tf_op jit(solution)/shard_map/dynamic_slice | solution.py:12
  9.7 2.5 %gather_fusion.1 = bf16[256]{0:T(256)(128)(2,1)S(1)} fusion(bf16[256,256]{1,0:T(8,128)(2,1)S(1)} %constant_dynamic-slice_fusion, s32[256]{0:T(256)S(1)} %bitcast.5), kind=kCustom, calls=%fused_computation.1 | custom fusion | bytes 3072 | tf_op jit(solution)/shard_map/jit(diagonal)/cond/branch_0_fun/gather | solution.py:13
  12.2 13.7 %all-gather = s32[8,1,256]{2,1,0:T(1,128)S(1)} all-gather(s32[1,1,256]{2,1,0:T(1,128)} %bitcast.7), channel_id=1, replica_groups=mesh['perm'=2,'subj'=8,'vert'=2] {'subj'}, dimensions={0}, use_global_device_ids=true | all-gather | bytes 9216 | tf_op jit(solution)/shard_map/all_gather | solution.py:11
  26.0 8.0 %scatter_custom_fusion = s32[2048]{0:T(1024)S(1)} fusion(s32[2048]{0:T(1024)S(1)} %compare_select_fusion.1, s32[2048]{0:T(1024)S(1)} %iota.16, s32[]{:T(128)} %constant.12.clone.1), kind=kCustom, calls=%fused_computation.20 | custom fusion | bytes 8196 | tf_op jit(solution)/shard_map/scatter | solution.py:17
  34.0 0.0 copy-start
  34.0 0.0 copy-start.1
  34.0 7.5 %gather_fusion = bf16[2048,256]{1,0:T(8,128)(2,1)S(1)} fusion(bf16[256,2048]{0,1:T(8,128)(2,1)S(1)} %copy.6, s32[2048]{0:T(1024)S(1)} %fusion.7), kind=kCustom, calls=%fused_computation | custom fusion | bytes 2105344 | tf_op jit(solution)/shard_map/jit(_take)/gather | solution.py:19
  41.5 0.0 copy-done
  41.6 0.1 multiply_reduce_fusion
  41.7 16.9 %all-gather.3.cloned.1.call-done = bf16[2048,1024]{1,0:T(8,128)(2,1)} async-done(((bf16[256,1024]{1,0:T(8,128)(2,1)}), bf16[2048,1024]{1,0:T(8,128)(2,1)}) %all-gather.3.cloned.1.call-update) | async-done | bytes 4194320 | tf_op jit(solution)/shard_map/all_gather | solution.py:20
  58.6 0.0 copy-done.1
  58.6 0.0 copy-start.2
  58.6 3.6 %fusion.1 = bf16[256,1024]{1,0:T(8,128)(2,1)S(1)} fusion(bf16[2048,1024]{1,0:T(8,128)(2,1)} %all-gather.3.cloned.1.call-done, s32[256]{0:T(256)S(1)} %copy-done.1), kind=kOutput, calls=%fused_computation.8 | convolution fusion | flops 1074528256 | bytes 4719616 | tf_op jit(solution)/shard_map/dot_general | solution.py:25
  62.2 0.0 copy-done.2
  62.2 1.5 %fusion.2 = f32[1024]{0:T(1024)S(1)} fusion(bf16[2048,1024]{1,0:T(8,128)(2,1)S(1)} %copy-done.2, bf16[256,1024]{1,0:T(8,128)(2,1)S(1)} %fusion.1, bf16[2048,256]{1,0:T(8,128)(2,1)S(1)} %gather_fusion, pred[2048]{0:T(1024)(128)(4,1)S(1)} %compare_and_fusion, f32[256]{0:T(256)S(1)} %convert_element_type.19), kind=kOutput, calls=%fused_computation.9 | convolution fusion | flops 1075575808 | bytes 5774336 | tf_op jit(solution)/shard_map/dot_general | solution.py:24
  63.7 15.1 %all-reduce = (f32[1024]{0:T(1024)S(1)}, f32[1024]{0:T(1024)S(1)}) all-reduce(f32[1024]{0:T(1024)S(1)} %fusion.2, f32[1024]{0:T(1024)S(1)} %multiply_reduce_fusion), channel_id=1, replica_groups=mesh['perm'=2,'subj'=8,'vert'=2] {'subj'}, use_global_device_ids=true, to_apply=%region_2.3 | all-reduce | flops 2048 | bytes 16384 | tf_op jit(solution)/shard_map/psum | solution.py:31
  78.8 0.6 multiply_divide_fusion
  (6 shorter events, 0.0 us)
Async XLA Ops:
  6.5 52.0 %all-gather.3.cloned.1.call-start = ((), (), s32[]{:S(2)}) async-start(), calls=%async_computation | async-start | bytes 4718592 | tf_op jit(solution)/shard_map/all_gather | solution.py:20
  34.0 7.5 %copy-start = (bf16[256,1024]{1,0:T(8,128)(2,1)S(1)}, bf16[256,1024]{1,0:T(8,128)(2,1)}, u32[]{:S(2)}) copy-start(bf16[256,1024]{1,0:T(8,128)(2,1)} %param.4) | copy-start | bytes 1572868
  34.0 24.5 %copy-start.1 = (s32[256]{0:T(256)S(1)}, s32[256]{0:T(256)}, u32[]{:S(2)}) copy-start(s32[256]{0:T(256)} %param.5) | copy-start | bytes 3076
  58.6 3.6 %copy-start.2 = (bf16[2048,1024]{1,0:T(8,128)(2,1)S(1)}, bf16[2048,1024]{1,0:T(8,128)(2,1)}, u32[]{:S(2)}) copy-start(bf16[2048,1024]{1,0:T(8,128)(2,1)} %all-gather.3.cloned.1.call-done) | copy-start | bytes 12582916
Sparse Core Ops, SparseCore 0:
  8.9 49.5 all-gather.2
where the time goes:
time: 86.4 us; the launch traced here: 86.2 us
  blocking collectives  28.8 us (33%)
  local copies, waits for them, and re-layouts  20.5 us (24%)
  waiting for transfers between devices  17.6 us (20%)
  between operations  13.5 us (16%)
  matrix products  5.08 us (6%)
    all_gather x1, waiting for transfers between devices, per_device(): piece = lax.all_gather(phenotype, 'subj', axis=0, tiled=True)  16.9 us
    psum x1, blocking collectives, per_device(): cross_all, squares_all = lax.psum((cross_term, squares), 'subj')  15.1 us
    all_gather x1, blocking collectives, per_device(): shuffle_all = lax.all_gather(shuffle, 'subj', axis=0, tiled=True)  13.7 us
    scatter x1, local copies, waits for them, and re-layouts, per_device(): inverse = jnp.zeros((subject_count,), jnp.int32).at[shuffle_all].set(jnp....  8.05 us
    gather x1, local copies, waits for them, and re-layouts, per_device(): kin_moved = jnp.take(kinship, inverse, axis=1)  7.5 us
    dot_general x1, matrix products, per_device(): picked = jnp.dot(picker, piece, preferred_element_type=jnp.float32)  3.62 us
    gather x1, local copies, waits for them, and re-layouts, per_device(): kin_diag = jnp.diagonal(own_block).astype(jnp.float32)  2.49 us
  transfers between devices with their start and end apart: 1, of which 1 were waited for; matrix products, arithmetic and copies ran while one was open for 24% of the time, Pallas kernels for 0%

commit v1 on v0

--- a/solution.py
+++ b/solution.py
@@ -2,6 +2,16 @@
 import jax.numpy as jnp
 from jax import lax
 from jax.sharding import PartitionSpec as P
+
+
+def gather_by_hops(array, name, d):
+    n_dev = lax.axis_size(name)
+    moving, shards = (array, [array])
+    for _ in range(n_dev - 1):
+        moving = lax.ppermute(moving, name, [(i, (i + 1) % n_dev) for i in range(n_dev)])
+        shards.insert(0, moving)
+    flat = jnp.concatenate(shards, axis=d)
+    return jnp.roll(flat, (lax.axis_index(name) + 1) * array.shape[d], axis=d)
 
 
 def per_device(kinship, phenotype, shuffle):
@@ -17,7 +27,7 @@
         .set(jnp.arange(subject_count, dtype=jnp.int32))
     )
     kin_moved = jnp.take(kinship, inverse, axis=1)
-    piece = lax.all_gather(phenotype, "subj", axis=0, tiled=True)
+    piece = gather_by_hops(phenotype, "subj", 0)
     piece_rows = piece.shape[0]
     targets = jnp.arange(piece_rows, dtype=jnp.int32)
     picker = (shuffle[:, None] == targets[None, :]).astype(jnp.bfloat16)

time: 86.4 us -> 116 us (1.34)
  waiting for transfers between devices: 17.6 us -> 54.3 us
  between operations: 13.5 us -> 0.23 us
  local copies, waits for them, and re-layouts: 20.5 us -> 30.7 us
  blocking collectives: 28.8 us -> 26.3 us
  matrix products: 5.08 us -> 2.79 us
    ppermute x0 -> x7, waiting for transfers between devices: none -> 54.3 us  [gather_by_hops(): lax.ppermute(moving, name, [(i, (i + 1) % n_dev) for i in range(n_dev)])]
    all_gather x1 -> x0, waiting for transfers between devices: 16.9 us -> none  [per_device(): piece = lax.all_gather(phenotype, 'subj', axis=0, tiled=True)]
    unnamed x7 -> x26, local copies, waits for them, and re-layouts: 1.5 us -> 10.2 us
    all_gather x1, blocking collectives: 13.7 us -> 10.4 us  [per_device(): shuffle_all = lax.all_gather(shuffle, 'subj', axis=0, tiled=True)]
    dot_general x1, matrix products: 3.62 us -> 1.34 us  [per_device(): picked = jnp.dot(picker, piece, preferred_element_type=jnp.float32)]
    gather x1, local copies, waits for them, and re-layouts: 7.5 us -> 9.02 us  [per_device(): kin_moved = jnp.take(kinship, inverse, axis=1)]
  transfers between devices with their start and end apart: 1 -> 7, of which waited for: 1 -> 6; matrix products, arithmetic and copies ran while one was open for 24% -> 19% of each run, Pallas kernels for 0% -> 0%
where the time goes in v1:
time: 116 us
  waiting for transfers between devices  54.3 us (47%)
  local copies, waits for them, and re-layouts  30.7 us (26%)
  blocking collectives  26.3 us (23%)
  matrix products  2.79 us (2%)
    ppermute x7, waiting for transfers between devices, gather_by_hops(): lax.ppermute(moving, name, [(i, (i + 1) % n_dev) for i in range(n_dev)])  54.3 us
    psum x1, blocking collectives, per_device(): cross_all, squares_all = lax.psum((cross_term, squares), 'subj')  15.9 us
    all_gather x1, blocking collectives, per_device(): shuffle_all = lax.all_gather(shuffle, 'subj', axis=0, tiled=True)  10.4 us
    unnamed x26, local copies, waits for them, and re-layouts  10.2 us
    gather x1, local copies, waits for them, and re-layouts, per_device(): kin_moved = jnp.take(kinship, inverse, axis=1)  9.02 us
    scatter x1, local copies, waits for them, and re-layouts, per_device(): inverse = jnp.zeros((subject_count,), jnp.int32).at[shuffle_all].set(jnp....  8.05 us
    gather x1, local copies, waits for them, and re-layouts, per_device(): kin_diag = jnp.diagonal(own_block).astype(jnp.float32)  2.49 us
  transfers between devices with their start and end apart: 7, of which 6 were waited for; matrix products, arithmetic and copies ran while one was open for 19% of the time, Pallas kernels for 0%

profile of v1, /device:TPU:0, one launch (start us, length us, event | category | flops | bytes accessed | tf_op | source)
XLA Modules:
  0.0 115.7 jit_solution(15502428397874545253)
XLA Ops:
  0.0 0.0 copy-start
  0.0 0.5 collective-permute-start
  0.5 11.2 %collective-permute-done = bf16[256,1024]{1,0:T(8,128)(2,1)S(1)} collective-permute-done((bf16[256,1024]{1,0:T(8,128)(2,1)}, bf16[256,1024]{1,0:T(8,128)(2,1)S(1)}, u32[]{:S(2)}, u32[]{:S(2)}) %collective-permute-start) | collective-permute-done | bytes 524320 | tf_op jit(solution)/shard_map/ppermute | solution.py:11
  11.7 0.0 collective-permute-start.1
  11.7 10.4 %collective-permute-done.1 = bf16[256,1024]{1,0:T(8,128)(2,1)S(1)} collective-permute-done((bf16[256,1024]{1,0:T(8,128)(2,1)S(1)}, bf16[256,1024]{1,0:T(8,128)(2,1)S(1)}, u32[]{:S(2)}, u32[]{:S(2)}) %collective-permute-start.1) | collective-permute-done | bytes 524320 | tf_op jit(solution)/shard_map/ppermute | solution.py:11
  22.1 0.0 collective-permute-start.2
  22.1 10.4 %collective-permute-done.2 = bf16[256,1024]{1,0:T(8,128)(2,1)S(1)} collective-permute-done((bf16[256,1024]{1,0:T(8,128)(2,1)S(1)}, bf16[256,1024]{1,0:T(8,128)(2,1)S(1)}, u32[]{:S(2)}, u32[]{:S(2)}) %collective-permute-start.2) | collective-permute-done | bytes 524320 | tf_op jit(solution)/shard_map/ppermute | solution.py:11
  32.5 0.0 collective-permute-start.3
  32.5 10.4 %collective-permute-done.3 = bf16[256,1024]{1,0:T(8,128)(2,1)S(1)} collective-permute-done((bf16[256,1024]{1,0:T(8,128)(2,1)S(1)}, bf16[256,1024]{1,0:T(8,128)(2,1)S(1)}, u32[]{:S(2)}, u32[]{:S(2)}) %collective-permute-start.3) | collective-permute-done | bytes 524320 | tf_op jit(solution)/shard_map/ppermute | solution.py:11
  42.9 0.0 copy-start.1
  42.9 0.8 copy-done.1
  43.7 0.0 collective-permute-start.4
  43.7 10.5 %collective-permute-done.4 = bf16[256,1024]{1,0:T(8,128)(2,1)} collective-permute-done((bf16[256,1024]{1,0:T(8,128)(2,1)S(1)}, bf16[256,1024]{1,0:T(8,128)(2,1)}, u32[]{:S(2)}, u32[]{:S(2)}) %collective-permute-start.4) | collective-permute-done | bytes 524320 | tf_op jit(solution)/shard_map/ppermute | solution.py:11
  54.2 0.0 collective-permute-start.5
  54.2 1.5 %copy.6 = bf16[256,2048]{0,1:T(8,128)(2,1)S(1)} copy(bf16[256,2048]{1,0:T(8,128)(2,1)} %param.3) | data formatting | bytes 2097152 | tf_op args[0]
  55.7 0.9 constant_dynamic-slice_fusion
  56.6 2.5 %gather_fusion.1 = bf16[256]{0:T(256)(128)(2,1)S(1)} fusion(bf16[256,256]{1,0:T(8,128)(2,1)S(1)} %constant_dynamic-slice_fusion, s32[256]{0:T(256)S(1)} %bitcast.3), kind=kCustom, calls=%fused_computation.1 | custom fusion | bytes 3072 | tf_op jit(solution)/shard_map/jit(diagonal)/cond/branch_0_fun/gather | solution.py:23
  59.1 10.4 %all-gather = s32[8,1,256]{2,1,0:T(1,128)S(1)} all-gather(s32[1,1,256]{2,1,0:T(1,128)} %bitcast.5), channel_id=1, replica_groups=mesh['perm'=2,'subj'=8,'vert'=2] {'subj'}, dimensions={0}, use_global_device_ids=true | all-gather | bytes 9216 | tf_op jit(solution)/shard_map/all_gather | solution.py:21
  69.5 8.0 %scatter_custom_fusion = s32[2048]{0:T(1024)S(1)} fusion(s32[2048]{0:T(1024)S(1)} %compare_select_fusion.1, s32[2048]{0:T(1024)S(1)} %iota.16, s32[]{:T(128)} %constant.55.clone.1), kind=kCustom, calls=%fused_computation.39 | custom fusion | bytes 8196 | tf_op jit(solution)/shard_map/scatter | solution.py:27
  77.6 0.0 collective-permute-done.5
  77.6 0.2 collective-permute-start.6
  77.8 9.0 %gather_fusion = bf16[2048,256]{1,0:T(8,128)(2,1)} fusion(bf16[256,2048]{0,1:T(8,128)(2,1)S(1)} %copy.6, s32[2048]{0:T(1024)S(1)} %fusion.19), kind=kCustom, calls=%fused_computation | custom fusion | bytes 2105344 | tf_op jit(solution)/shard_map/jit(_take)/gather | solution.py:29
  86.8 0.0 copy-done
  86.8 0.0 copy-start.2
  86.8 0.1 multiply_reduce_fusion
  87.0 0.0 copy-start.4
  87.0 1.4 %collective-permute-done.6 = bf16[256,1024]{1,0:T(8,128)(2,1)} collective-permute-done((bf16[256,1024]{1,0:T(8,128)(2,1)}, bf16[256,1024]{1,0:T(8,128)(2,1)}, u32[]{:S(2)}, u32[]{:S(2)}) %collective-permute-start.6) | collective-permute-done | bytes 524320 | tf_op jit(solution)/shard_map/ppermute | solution.py:11
  88.4 1.1 constant_dynamic-update-slice_fusion.15
  89.4 1.1 constant_dynamic-update-slice_fusion.14
  90.5 1.1 constant_dynamic-update-slice_fusion.13
  91.6 1.1 constant_dynamic-update-slice_fusion.12
  92.8 0.0 copy-start.3
  92.9 1.2 constant_dynamic-update-slice_fusion.7
  94.0 1.1 constant_dynamic-update-slice_fusion.6
  95.1 1.1 constant_dynamic-update-slice_fusion.5
  96.2 0.0 copy-done.2
  96.4 0.0 copy-done.4
  96.4 1.3 %fusion.9 = bf16[256,1024]{1,0:T(8,128)(2,1)S(1)} fusion(bf16[4096,1024]{1,0:T(8,128)(2,1)S(1)} %constant_dynamic-update-slice_fusion, s32[]{:T(128)S(6)} %select_n.33, s32[256]{0:T(256)S(1)} %copy-done.4), kind=kOutput, calls=%fused_computation.11 | convolution fusion | flops 1074528256 | bytes 4719620 | tf_op jit(solution)/shard_map/dot_general | solution.py:35
  97.8 0.0 copy-done.3
  97.8 1.4 %fusion.12 = f32[1024]{0:T(1024)S(1)} fusion(bf16[4096,1024]{1,0:T(8,128)(2,1)S(1)} %constant_dynamic-update-slice_fusion, s32[]{:T(128)S(6)} %select_n.33, bf16[256,1024]{1,0:T(8,128)(2,1)S(1)} %fusion.9, bf16[2048,256]{1,0:T(8,128)(2,1)S(1)} %copy-done.3, pred[2048]{0:T(1024)(128)(4,1)S(1)} %compare_and_fusion, f32[256]{0:T(256)S(1)} %convert_element_type.19), kind=kOutput, calls=%fused_computation.12 | convolution fusion | flops 1075575808 | bytes 5774340 | tf_op jit(solution)/shard_map/dot_general | solution.py:34
  99.2 15.9 %all-reduce = (f32[1024]{0:T(1024)S(1)}, f32[1024]{0:T(1024)S(1)}) all-reduce(f32[1024]{0:T(1024)S(1)} %fusion.12, f32[1024]{0:T(1024)S(1)} %multiply_reduce_fusion), channel_id=1, replica_groups=mesh['perm'=2,'subj'=8,'vert'=2] {'subj'}, use_global_device_ids=true, to_apply=%region_2.3 | all-reduce | flops 2048 | bytes 16384 | tf_op jit(solution)/shard_map/psum | solution.py:41
  115.1 0.6 multiply_divide_fusion
  (15 shorter events, 0.4 us)
Async XLA Ops:
  0.0 86.8 %copy-start = (bf16[256,1024]{1,0:T(8,128)(2,1)S(1)}, bf16[256,1024]{1,0:T(8,128)(2,1)}, u32[]{:S(2)}) copy-start(bf16[256,1024]{1,0:T(8,128)(2,1)} %param.4) | copy-start | bytes 1572868
  0.0 11.7 %collective-permute-start = (bf16[256,1024]{1,0:T(8,128)(2,1)}, bf16[256,1024]{1,0:T(8,128)(2,1)S(1)}, u32[]{:S(2)}, u32[]{:S(2)}) collective-permute-start(bf16[256,1024]{1,0:T(8,128)(2,1)} %param.4), channel_id=1, source_target_pairs={{0,2},{2,4},{4,6},{6,8},{8,10},{10,12},{12,14},{14,0},{1,3},{3,5},... | collective-permute-start | bytes 1572872 | tf_op jit(solution)/shard_map/ppermute | solution.py:11
  11.7 10.4 %collective-permute-start.1 = (bf16[256,1024]{1,0:T(8,128)(2,1)S(1)}, bf16[256,1024]{1,0:T(8,128)(2,1)S(1)}, u32[]{:S(2)}, u32[]{:S(2)}) collective-permute-start(bf16[256,1024]{1,0:T(8,128)(2,1)S(1)} %collective-permute-done), channel_id=1, source_target_pairs={{0,2},{2,4},{4,6},{6,8},{8,10},{10,12},{12,14},{14,0},{1,3},{3,5},... | collective-permute-start | bytes 1572872 | tf_op jit(solution)/shard_map/ppermute | solution.py:11
  22.1 10.4 %collective-permute-start.2 = (bf16[256,1024]{1,0:T(8,128)(2,1)S(1)}, bf16[256,1024]{1,0:T(8,128)(2,1)S(1)}, u32[]{:S(2)}, u32[]{:S(2)}) collective-permute-start(bf16[256,1024]{1,0:T(8,128)(2,1)S(1)} %collective-permute-done.1), channel_id=1, source_target_pairs={{0,2},{2,4},{4,6},{6,8},{8,10},{10,12},{12,14},{14,0},{1,3},{3,5},... | collective-permute-start | bytes 1572872 | tf_op jit(solution)/shard_map/ppermute | solution.py:11
  32.5 10.4 %collective-permute-start.3 = (bf16[256,1024]{1,0:T(8,128)(2,1)S(1)}, bf16[256,1024]{1,0:T(8,128)(2,1)S(1)}, u32[]{:S(2)}, u32[]{:S(2)}) collective-permute-start(bf16[256,1024]{1,0:T(8,128)(2,1)S(1)} %collective-permute-done.2), channel_id=1, source_target_pairs={{0,2},{2,4},{4,6},{6,8},{8,10},{10,12},{12,14},{14,0},{1,3},{3,5},... | collective-permute-start | bytes 1572872 | tf_op jit(solution)/shard_map/ppermute | solution.py:11
  42.9 0.8 copy-start.1
  43.7 10.5 %collective-permute-start.4 = (bf16[256,1024]{1,0:T(8,128)(2,1)S(1)}, bf16[256,1024]{1,0:T(8,128)(2,1)}, u32[]{:S(2)}, u32[]{:S(2)}) collective-permute-start(bf16[256,1024]{1,0:T(8,128)(2,1)S(1)} %collective-permute-done.3), channel_id=1, source_target_pairs={{0,2},{2,4},{4,6},{6,8},{8,10},{10,12},{12,14},{14,0},{1,3},{3,5},... | collective-permute-start | bytes 1572872 | tf_op jit(solution)/shard_map/ppermute | solution.py:11
  54.2 23.4 %collective-permute-start.5 = (bf16[256,1024]{1,0:T(8,128)(2,1)}, bf16[256,1024]{1,0:T(8,128)(2,1)}, u32[]{:S(2)}, u32[]{:S(2)}) collective-permute-start(bf16[256,1024]{1,0:T(8,128)(2,1)} %collective-permute-done.4), channel_id=1, source_target_pairs={{0,2},{2,4},{4,6},{6,8},{8,10},{10,12},{12,14},{14,0},{1,3},{3,5},... | collective-permute-start | bytes 1572872 | tf_op jit(solution)/shard_map/ppermute | solution.py:11
  77.6 10.8 %collective-permute-start.6 = (bf16[256,1024]{1,0:T(8,128)(2,1)}, bf16[256,1024]{1,0:T(8,128)(2,1)}, u32[]{:S(2)}, u32[]{:S(2)}) collective-permute-start(bf16[256,1024]{1,0:T(8,128)(2,1)} %collective-permute-done.5), channel_id=1, source_target_pairs={{0,2},{2,4},{4,6},{6,8},{8,10},{10,12},{12,14},{14,0},{1,3},{3,5},... | collective-permute-start | bytes 1572872 | tf_op jit(solution)/shard_map/ppermute | solution.py:11
  86.8 9.4 %copy-start.2 = (bf16[256,1024]{1,0:T(8,128)(2,1)S(1)}, bf16[256,1024]{1,0:T(8,128)(2,1)}, u32[]{:S(2)}) copy-start(bf16[256,1024]{1,0:T(8,128)(2,1)} %copy-done.1) | copy-start | bytes 1572868
  87.0 9.4 %copy-start.4 = (s32[256]{0:T(256)S(1)}, s32[256]{0:T(256)}, u32[]{:S(2)}) copy-start(s32[256]{0:T(256)} %param.5) | copy-start | bytes 3076
  92.8 5.0 %copy-start.3 = (bf16[2048,256]{1,0:T(8,128)(2,1)S(1)}, bf16[2048,256]{1,0:T(8,128)(2,1)}, u32[]{:S(2)}) copy-start(bf16[2048,256]{1,0:T(8,128)(2,1)} %gather_fusion) | copy-start | bytes 3145732
